TPU v7x, 128 devices: a whole 4x4x4 slice. The times are simulated.
128 devices in a mesh: tm: 16 (over z, x), tile: 8 (over y, core).
Axes of the slice: x: 4, y: 4, z: 4, core: 2. Of those that a mesh axis runs over, the one named last changes fastest.
Arguments:
- frames: bfloat16 [64, 64, 64, 128], P('tm', 'tile'), may hold values from -6 to 6
- cotangent: bfloat16 [64, 64, 64, 128], P('tm', 'tile'), may hold values from -6 to 6
- w_in: bfloat16 [3, 3, 128, 128], replicated, may hold values from -0.1875 to 0.1875
- w_out: bfloat16 [3, 3, 128, 128], replicated, may hold values from -0.1875 to 0.1875
- skip: float32 [128], replicated, may hold values from 0.5 to 1.5
- log_decay: float32 [64, 128], P('tm'), may hold values from -1 to 0
Outputs:
- output: bfloat16 [64, 64, 64, 128], P('tm', 'tile')
- grad_frames: bfloat16 [64, 64, 64, 128], P('tm', 'tile')
- grad_w_in: float32 [3, 3, 128, 128], replicated
- grad_w_out: float32 [3, 3, 128, 128], replicated
All inputs are finite; a program needn't handle non-finite values.
Results may differ from a plain program's by a relative error of at most 0.0029.
Values may be sent and summed in bfloat16 or wider, within the bound.
A program may use at most 64 MiB of HBM per device.

v0:
```python
import math

import jax
import jax.numpy as jnp
from jax import lax
from jax.sharding import PartitionSpec as P


def extended(block, sides, width):
    for axis, dim in sides:
        count = lax.axis_size(axis)
        forward = [(i, i + 1) for i in range(count - 1)]
        backward = [(target, source) for source, target in forward]
        low = lax.ppermute(
            lax.slice_in_dim(block, block.shape[dim] - width, None, axis=dim), axis, forward
        )
        high = lax.ppermute(lax.slice_in_dim(block, 0, width, axis=dim), axis, backward)
        block = jnp.concatenate([low, block, high], axis=dim)
    return block


def carried_in(value, axis, join, neutral, backward):
    count, mine = (lax.axis_size(axis), lax.axis_index(axis))
    pieces = jax.tree.map(lambda part: lax.all_gather(part, axis), value)
    if backward:
        pieces = jax.tree.map(lambda part: part[::-1], pieces)
        mine = count - 1 - mine
    so_far = jax.tree.map(
        lambda part, zero: jnp.full_like(part, 0) + jnp.asarray(zero, part.dtype), value, neutral
    )

    def hop(position, so_far):
        longer = join(so_far, jax.tree.map(lambda part: part[position], pieces))
        return jax.tree.map(lambda new, old: jnp.where(position < mine, new, old), longer, so_far)

    return lax.fori_loop(0, count - 1, hop, so_far)


def flipped(weight):
    return jnp.transpose(weight[::-1, ::-1], (0, 1, 3, 2))


def widen_cols(field):
    return jnp.pad(field, ((0, 0), (0, 0), (1, 1), (0, 0)))


def convolve(padded, weight):
    rows = padded.shape[1] - 2
    cols = padded.shape[2] - 2
    result = jnp.zeros((padded.shape[0], rows, cols, weight.shape[3]), jnp.float32)
    for row_off in range(3):
        for col_off in range(3):
            piece = padded[:, row_off : row_off + rows, col_off : col_off + cols, :].reshape(
                -1, weight.shape[2]
            )
            result = result + jnp.dot(
                piece, weight[row_off, col_off], preferred_element_type=jnp.float32
            ).reshape(result.shape)
    return result


def weight_grad(padded, target):
    rows = target.shape[1]
    cols = target.shape[2]
    flat = target.reshape(-1, target.shape[3])
    pieces = []
    for row_off in range(3):
        line = []
        for col_off in range(3):
            piece = padded[:, row_off : row_off + rows, col_off : col_off + cols, :].reshape(
                -1, padded.shape[3]
            )
            line.append(
                lax.dot_general(
                    piece, flat, (((0,), (0,)), ((), ())), preferred_element_type=jnp.float32
                )
            )
        pieces.append(jnp.stack(line))
    return jnp.stack(pieces)


def forward_combine(earlier, later):
    return (earlier[0] * later[0], later[0] * earlier[1] + later[1])


def backward_combine(earlier, later):
    return (later[0] * earlier[0], later[1] + later[0] * earlier[1])


def shards(frames, cotangent, w_in, w_out, skip, log_decay):
    decay = jnp.exp(log_decay)
    frames_padded = widen_cols(extended(frames, (("tile", 1),), 1))
    drive = convolve(frames_padded, w_in)
    cot_padded = widen_cols(extended(cotangent, (("tile", 1),), 1))
    state_grad = convolve(cot_padded, flipped(w_out))

    def advance(state, item):
        rate, inflow = item
        state = rate * state + (1.0 - rate) * inflow
        return (state, state)

    blank = jnp.zeros(drive.shape[1:], jnp.float32)
    _, local_states = lax.scan(advance, blank, (decay, drive))
    cumulative = jnp.cumsum(log_decay, axis=0)
    whole_decay = jnp.exp(cumulative[-1])
    reach = jnp.exp(cumulative)
    tail = jnp.exp(cumulative[-1][None, :] - cumulative)

    def retreat(carry, item):
        rate, grad_here = item
        adjoint = grad_here + carry
        return (rate * adjoint, adjoint)

    outflow, local_adjoints = lax.scan(retreat, blank, (decay, state_grad), reverse=True)
    identity = (jnp.ones_like(whole_decay), blank)
    incoming_state = carried_in(
        (whole_decay, local_states[-1]), "tm", forward_combine, identity, False
    )[1]
    incoming_adjoint = carried_in((whole_decay, outflow), "tm", backward_combine, identity, True)[1]
    states = local_states + reach[:, None, None, :] * incoming_state[None]
    states_bf = states.astype(jnp.bfloat16)
    states_padded = widen_cols(extended(states_bf, (("tile", 1),), 1))
    output = (convolve(states_padded, w_out) + skip * frames.astype(jnp.float32)).astype(
        jnp.bfloat16
    )
    factor = 1.0 / math.sqrt(
        frames.shape[0]
        * lax.axis_size("tm")
        * frames.shape[1]
        * lax.axis_size("tile")
        * frames.shape[2]
    )
    out_partial = weight_grad(states_padded, cotangent)
    adjoints = local_adjoints + tail[:, None, None, :] * incoming_adjoint[None]
    inflow_wide = ((1.0 - decay)[:, None, None, :] * adjoints).astype(jnp.bfloat16)
    inflow_padded = widen_cols(extended(inflow_wide, (("tile", 1),), 1))
    grad_frames = (
        convolve(inflow_padded, flipped(w_in)) + skip * cotangent.astype(jnp.float32)
    ).astype(jnp.bfloat16)
    in_partial = weight_grad(frames_padded, inflow_wide)
    in_summed, out_summed = lax.psum((in_partial, out_partial), ("tm", "tile"))
    return (output, grad_frames, in_summed * factor, out_summed * factor)


def solution(mesh):
    placed = (
        P("tm", "tile", None, None),
        P("tm", "tile", None, None),
        P(),
        P(),
        P(),
        P("tm", None),
    )
    return jax.shard_map(
        shards,
        mesh=mesh,
        in_specs=placed,
        out_specs=(P("tm", "tile", None, None), P("tm", "tile", None, None), P(), P()),
        check_vma=False,
    )
```

profile of v0, /device:TPU:1, one launch (start us, length us, event | category | flops | bytes accessed | tf_op | source)
XLA Modules:
  0.0 349.0 jit_solution(3721453825366064998)
XLA Ops:
  8.2 4.6 %collective-permute-start = (bf16[4,1,64,128]{3,2,1,0:T(8,128)(2,1)S(1)}, bf16[4,1,64,128]{3,2,1,0:T(8,128)(2,1)S(1)}, u32[]{:S(2)}, u32[]{:S(2)}) collective-permute-start(bf16[4,1,64,128]{3,2,1,0:T(8,128)(2,1)S(1)} %get-tuple-element.454), channel_id=1, source_target_pairs={{0,1},{1,2},{2,3},{3,4},{4,5},{5,6},{6,7},{8,9},{9,10},{10,11},{11... | collective-permute-start | bytes 196616 | tf_op jit(solution)/shard_map/ppermute | solution.py:14
  12.8 1.9 collective-permute-start.1
  15.4 1.4 constant_dynamic-update-slice_fusion
  16.9 1.5 collective-permute-done.1
  21.3 1.3 fusion.15
  22.6 1.1 broadcast.32.clone
  23.7 7.2 %while.58 = (s32[]{:T(128)}, f32[8,64,128]{2,1,0:T(8,128)S(1)}, f32[4,8,64,128]{3,2,1,0:T(8,128)}, f32[4,128]{1,0:T(4,128)S(1)}, f32[4,8,64,128]{3,2,1,0:T(8,128)}, /*index=5*/s32[]{:T(128)}, s32[]{:T(128)}) while((s32[]{:T(128)}, f32[8,64,128]{2,1,0:T(8,128)S(1)}, f32[4,8,64,128]{3,2,1,0:T(8,128)}, f32[4,128]{1,0:T(4,128)S(1)}, ...), condition=%wide.region_1.2_spmd.clone, body=%wide.region_0.1_spmd.clone.sunk | while | flops 262275 | bytes 1051239 | solution.py:103
  23.7 1.9 bitcast_dynamic-update-slice_fusion.4
  25.6 1.8 bitcast_dynamic-update-slice_fusion.4
  27.3 1.8 bitcast_dynamic-update-slice_fusion.4
  29.1 1.8 bitcast_dynamic-update-slice_fusion.4
  30.9 1.7 slice.297
  32.7 2.2 collective-permute-start.4
  34.9 2.1 collective-permute-start.5
  37.0 1.2 copy.13
  38.3 2.2 collective-permute-done.5
  43.1 1.3 fusion.10
  45.5 11.1 %while.60 = (s32[]{:T(128)}, f32[8,64,128]{2,1,0:T(8,128)S(1)}, f32[4,8,64,128]{3,2,1,0:T(8,128)}, f32[4,128]{1,0:T(4,128)S(1)}, f32[4,8,64,128]{3,2,1,0:T(8,128)}, /*index=5*/s32[]{:T(128)}, s32[]{:T(128)}, s32[]{:T(128)}) while((s32[]{:T(128)}, f32[8,64,128]{2,1,0:T(8,128)S(1)}, f32[4,8,64,128]{3,2,1,0:T(8,128)}, ...), condition=%wide.region_6.7_spmd.clone, body=%wide.region_5.6_spmd.clone.sunk | while | flops 327684 | bytes 1574528 | solution.py:114
  45.5 1.7 bitcast_dynamic-update-slice_fusion.5
  48.3 1.7 bitcast_dynamic-update-slice_fusion.5
  51.1 1.7 bitcast_dynamic-update-slice_fusion.5
  53.8 1.7 bitcast_dynamic-update-slice_fusion.5
  57.7 19.5 %all-gather.1 = f32[16,1,128]{2,1,0:T(1,128)S(1)} all-gather(f32[1,1,128]{2,1,0:T(1,128)S(1)} %get-tuple-element.461), channel_id=1, replica_groups=mesh['tm'=16,'tile'=8] {'tm'}, dimensions={0}, use_global_device_ids=true | all-gather | bytes 8704 | tf_op jit(solution)/shard_map/all_gather | solution.py:24
  77.9 7.9 %all-gather.5.cloned.1.call-done = f32[16,8,64,128]{3,2,1,0:T(8,128)} async-done(((f32[1,8,64,128]{3,2,1,0:T(8,128)}), f32[16,8,64,128]{3,2,1,0:T(8,128)}) %all-gather.5.cloned.1.call-update) | async-done | bytes 4194320 | tf_op jit(solution)/shard_map/all_gather | solution.py:24
  85.8 17.9 %while.59 = (s32[]{:T(128)}, f32[8,64,128]{2,1,0:T(8,128)S(1)}, s32[]{:T(128)}, f32[16,128]{1,0:T(8,128)S(1)}, f32[16,8,64,128]{3,2,1,0:T(8,128)}, /*index=5*/s32[]{:T(128)}, s32[]{:T(128)}) while((s32[]{:T(128)}, f32[8,64,128]{2,1,0:T(8,128)S(1)}, s32[]{:T(128)}, f32[16,128]{1,0:T(8,128)S(1)}, f32[16,8,64,128]{3,2,1,0:T(8,128)}, ...), condition=%wide.region_4.5_spmd.clone, body=%wide.region_3.4_spmd.clone.sunk | while | flops 262148 | bytes 788081 | solution.py:36
  85.8 1.1 fusion.164
  87.0 1.2 fusion.164
  88.2 1.2 fusion.164
  89.4 1.2 fusion.164
  90.5 1.2 fusion.164
  91.7 1.2 fusion.164
  92.9 1.2 fusion.164
  94.1 1.2 fusion.164
  95.3 1.2 fusion.164
  96.5 1.2 fusion.164
  97.7 1.2 fusion.164
  98.9 1.2 fusion.164
  100.1 1.2 fusion.164
  101.3 1.2 fusion.164
  102.5 1.2 fusion.164
  103.7 1.4 add_convert_fusion
  106.1 33.3 %all-gather.7.cloned.1.call-done = f32[128,64,128]{2,1,0:T(8,128)} async-done(((f32[8,64,128]{2,1,0:T(8,128)}), f32[128,64,128]{2,1,0:T(8,128)}) %all-gather.7.cloned.1.call-update) | async-done | bytes 4194320 | tf_op jit(solution)/shard_map/all_gather | solution.py:24
  139.4 4.7 %rev.13 = f32[16,8,64,128]{3,2,1,0:T(8,128)} reverse(f32[16,8,64,128]{3,2,1,0:T(8,128)} %bitcast.460), dimensions={0} | reverse | bytes 8388608 | tf_op jit(solution)/shard_map/rev | solution.py:26
  144.2 17.0 %while.61 = (s32[]{:T(128)}, f32[8,64,128]{2,1,0:T(8,128)S(1)}, s32[]{:T(128)}, f32[16,8,64,128]{3,2,1,0:T(8,128)}, f32[16,128]{1,0:T(8,128)S(1)}, /*index=5*/s32[]{:T(128)}, s32[]{:T(128)}) while((s32[]{:T(128)}, f32[8,64,128]{2,1,0:T(8,128)S(1)}, s32[]{:T(128)}, f32[16,8,64,128]{3,2,1,0:T(8,128)}, f32[16,128]{1,0:T(8,128)S(1)}, ...), condition=%wide.region_8.9_spmd.clone, body=%wide.region_7.8_spmd.clone.sunk | while | flops 262148 | bytes 788081 | solution.py:36
  146.4 1.1 fusion.166
  148.7 1.1 fusion.166
  151.0 1.1 fusion.166
  153.3 1.1 fusion.166
  155.5 1.1 fusion.166
  156.7 1.1 fusion.166
  161.2 1.5 multiply_convert_fusion
  165.9 3.8 %collective-permute-start.2 = (bf16[4,1,64,128]{3,2,1,0:T(8,128)(2,1)}, bf16[4,1,64,128]{3,2,1,0:T(8,128)(2,1)S(1)}, u32[]{:S(2)}, u32[]{:S(2)}) collective-permute-start(bf16[4,1,64,128]{3,2,1,0:T(8,128)(2,1)} %get-tuple-element.450), channel_id=1, source_target_pairs={{0,1},{1,2},{2,3},{3,4},{4,5},{5,6},{6,7},{8,9},{9,10},{10,11},{11... | collective-permute-start | bytes 196616 | tf_op jit(solution)/shard_map/ppermute | solution.py:14
  169.7 1.9 collective-permute-start.3
  171.6 3.6 %collective-permute-start.6 = (bf16[4,1,64,128]{3,2,1,0:T(8,128)(2,1)S(1)}, bf16[4,1,64,128]{3,2,1,0:T(8,128)(2,1)S(1)}, u32[]{:S(2)}, u32[]{:S(2)}) collective-permute-start(bf16[4,1,64,128]{3,2,1,0:T(8,128)(2,1)S(1)} %get-tuple-element.446), channel_id=1, source_target_pairs={{0,1},{1,2},{2,3},{3,4},{4,5},{5,6},{6,7},{8,9},{9,10},{10,11},{11... | collective-permute-start | bytes 196616 | tf_op jit(solution)/shard_map/ppermute | solution.py:14
  175.3 2.1 collective-permute-start.7
  180.6 1.3 fusion.54
  183.4 1.3 convolution_add_fusion.13
  185.6 1.3 fusion.39
  188.3 1.3 convolution_add_fusion.1
  192.7 2.5 fusion.16
  195.2 1.1 fusion.35
  196.4 2.0 fusion.17
  198.4 141.2 %all-reduce.7.cloned.1.call-done = (f32[3,3,128,128]{3,2,1,0:T(8,128)}, f32[3,3,128,128]{3,2,1,0:T(8,128)}) async-done(((f32[3,3,128,128]{3,2,1,0:T(8,128)}, f32[3,3,128,128]{3,2,1,0:T(8,128)}), (f32[3,3,128,128]{3,2,1,0:T(8,128)}, f32[3,3,128,128]{3,2,1,0:T(8,128)})) %all-reduce.7.cloned.1.call-update) | async-done | bytes 1179664 | tf_op jit(solution)/shard_map/psum | solution.py:141
  339.6 2.0 broadcast_multiply_fusion.2
  (172 shorter events, 39.4 us)
Async XLA Ops:
  7.2 11.2 %copy-start.2 = (bf16[4,8,64,128]{3,2,1,0:T(8,128)(2,1)S(1)}, bf16[4,8,64,128]{3,2,1,0:T(8,128)(2,1)}, u32[]{:S(2)}) copy-start(bf16[4,8,64,128]{3,2,1,0:T(8,128)(2,1)} %param.14) | copy-start | bytes 1572868
  7.2 78.6 %all-gather.5.cloned.1.call-start = ((), (), s32[]{:S(2)}) async-start(), calls=%async_computation | async-start | bytes 4456448 | tf_op jit(solution)/shard_map/all_gather | solution.py:24
  8.2 7.2 %collective-permute-start = (bf16[4,1,64,128]{3,2,1,0:T(8,128)(2,1)S(1)}, bf16[4,1,64,128]{3,2,1,0:T(8,128)(2,1)S(1)}, u32[]{:S(2)}, u32[]{:S(2)}) collective-permute-start(bf16[4,1,64,128]{3,2,1,0:T(8,128)(2,1)S(1)} %get-tuple-element.454), channel_id=1, source_target_pairs={{0,1},{1,2},{2,3},{3,4},{4,5},{5,6},{6,7},{8,9},{9,10},{10,11},{11... | collective-permute-start | bytes 196616 | tf_op jit(solution)/shard_map/ppermute | solution.py:14
  12.8 5.6 %collective-permute-start.1 = (bf16[4,1,64,128]{3,2,1,0:T(8,128)(2,1)S(1)}, bf16[4,1,64,128]{3,2,1,0:T(8,128)(2,1)S(1)}, u32[]{:S(2)}, u32[]{:S(2)}) collective-permute-start(bf16[4,1,64,128]{3,2,1,0:T(8,128)(2,1)S(1)} %get-tuple-element.455), channel_id=1, source_target_pairs={{1,0},{2,1},{3,2},{4,3},{5,4},{6,5},{7,6},{9,8},{10,9},{11,10},{12... | collective-permute-start | bytes 196616 | tf_op jit(solution)/shard_map/ppermute | solution.py:17
  15.4 3.3 copy-start.11
  16.9 2.4 copy-start.9
  19.0 0.8 copy-start.4
  23.7 9.0 %copy-start.1 = (bf16[4,8,64,128]{3,2,1,0:T(8,128)(2,1)S(1)}, bf16[4,8,64,128]{3,2,1,0:T(8,128)(2,1)}, u32[]{:S(2)}) copy-start(bf16[4,8,64,128]{3,2,1,0:T(8,128)(2,1)} %param.15) | copy-start | bytes 1572868
  32.6 106.8 %all-gather.7.cloned.1.call-start = ((), (), s32[]{:S(2)}) async-start(), calls=%async_computation.1 | async-start | bytes 4456448 | tf_op jit(solution)/shard_map/all_gather | solution.py:24
  32.7 5.6 %collective-permute-start.4 = (bf16[4,1,64,128]{3,2,1,0:T(8,128)(2,1)S(1)}, bf16[4,1,64,128]{3,2,1,0:T(8,128)(2,1)S(1)}, u32[]{:S(2)}, u32[]{:S(2)}) collective-permute-start(bf16[4,1,64,128]{3,2,1,0:T(8,128)(2,1)S(1)} %get-tuple-element.448), channel_id=1, source_target_pairs={{0,1},{1,2},{2,3},{3,4},{4,5},{5,6},{6,7},{8,9},{9,10},{10,11},{11... | collective-permute-start | bytes 196616 | tf_op jit(solution)/shard_map/ppermute | solution.py:14
  34.9 5.6 %collective-permute-start.5 = (bf16[4,1,64,128]{3,2,1,0:T(8,128)(2,1)S(1)}, bf16[4,1,64,128]{3,2,1,0:T(8,128)(2,1)S(1)}, u32[]{:S(2)}, u32[]{:S(2)}) collective-permute-start(bf16[4,1,64,128]{3,2,1,0:T(8,128)(2,1)S(1)} %get-tuple-element.449), channel_id=1, source_target_pairs={{1,0},{2,1},{3,2},{4,3},{5,4},{6,5},{7,6},{9,8},{10,9},{11,10},{12... | collective-permute-start | bytes 196616 | tf_op jit(solution)/shard_map/ppermute | solution.py:17
  45.5 12.1 %copy-start.15 = (f32[4,128]{1,0:T(4,128)S(1)}, f32[4,128]{1,0:T(4,128)}, u32[]{:S(2)}) copy-start(f32[4,128]{1,0:T(4,128)} %param.19) | copy-start | bytes 6148
  56.6 0.7 copy-start
  57.3 282.3 %all-reduce.7.cloned.1.call-start = ((), (), s32[]{:S(2)}) async-start(), calls=%async_computation.2 | async-start | bytes 2359296 | tf_op jit(solution)/shard_map/psum | solution.py:141
  161.2 1.5 copy-start.5
  161.2 1.9 copy-start.10
  165.9 12.5 %collective-permute-start.2 = (bf16[4,1,64,128]{3,2,1,0:T(8,128)(2,1)}, bf16[4,1,64,128]{3,2,1,0:T(8,128)(2,1)S(1)}, u32[]{:S(2)}, u32[]{:S(2)}) collective-permute-start(bf16[4,1,64,128]{3,2,1,0:T(8,128)(2,1)} %get-tuple-element.450), channel_id=1, source_target_pairs={{0,1},{1,2},{2,3},{3,4},{4,5},{5,6},{6,7},{8,9},{9,10},{10,11},{11... | collective-permute-start | bytes 196616 | tf_op jit(solution)/shard_map/ppermute | solution.py:14
  169.7 8.6 %collective-permute-start.3 = (bf16[4,1,64,128]{3,2,1,0:T(8,128)(2,1)}, bf16[4,1,64,128]{3,2,1,0:T(8,128)(2,1)S(1)}, u32[]{:S(2)}, u32[]{:S(2)}) collective-permute-start(bf16[4,1,64,128]{3,2,1,0:T(8,128)(2,1)} %get-tuple-element.451), channel_id=1, source_target_pairs={{1,0},{2,1},{3,2},{4,3},{5,4},{6,5},{7,6},{9,8},{10,9},{11,10},{12... | collective-permute-start | bytes 196616 | tf_op jit(solution)/shard_map/ppermute | solution.py:17
  171.6 13.3 %collective-permute-start.6 = (bf16[4,1,64,128]{3,2,1,0:T(8,128)(2,1)S(1)}, bf16[4,1,64,128]{3,2,1,0:T(8,128)(2,1)S(1)}, u32[]{:S(2)}, u32[]{:S(2)}) collective-permute-start(bf16[4,1,64,128]{3,2,1,0:T(8,128)(2,1)S(1)} %get-tuple-element.446), channel_id=1, source_target_pairs={{0,1},{1,2},{2,3},{3,4},{4,5},{5,6},{6,7},{8,9},{9,10},{10,11},{11... | collective-permute-start | bytes 196616 | tf_op jit(solution)/shard_map/ppermute | solution.py:14
  175.3 9.7 %collective-permute-start.7 = (bf16[4,1,64,128]{3,2,1,0:T(8,128)(2,1)S(1)}, bf16[4,1,64,128]{3,2,1,0:T(8,128)(2,1)S(1)}, u32[]{:S(2)}, u32[]{:S(2)}) collective-permute-start(bf16[4,1,64,128]{3,2,1,0:T(8,128)(2,1)S(1)} %get-tuple-element.447), channel_id=1, source_target_pairs={{1,0},{2,1},{3,2},{4,3},{5,4},{6,5},{7,6},{9,8},{10,9},{11,10},{12... | collective-permute-start | bytes 196616 | tf_op jit(solution)/shard_map/ppermute | solution.py:17
  179.7 1.0 copy-start.12
  184.6 1.0 copy-start.13
  191.2 0.7 copy-start.16
  191.3 1.0 copy-start.3
  191.3 1.4 copy-start.6
  192.7 3.7 %copy-start.8 = (f32[4,8,64,128]{3,2,1,0:T(8,128)S(1)}, f32[4,8,64,128]{3,2,1,0:T(8,128)}, u32[]{:S(2)}) copy-start(f32[4,8,64,128]{3,2,1,0:T(8,128)} %convolution_add_fusion.1) | copy-start | bytes 3145732
  195.2 1.2 copy-start.7
  339.6 2.0 copy-start.14
Sparse Core Ops, SparseCore 0:
  32.7 53.0 all-gather.4
  88.5 50.9 all-gather.6
  191.4 148.1 all-reduce.6
where the time goes:
time: 351 us; the launch traced here: 349 us
  waiting for transfers between devices  186 us (53%)
  other arithmetic  61.5 us (18%)
  matrix products  27.2 us (8%)
  starting transfers between devices  22.5 us (6%)
  blocking collectives  19.5 us (6%)
  local copies, waits for them, and re-layouts  16.9 us (5%)
  between operations  14.4 us (4%)
    psum x1, waiting for transfers between devices, shards(): in_summed, out_summed = lax.psum((in_partial, out_partial), ('tm', 'tile'))  141 us
    all_gather x2, waiting for transfers between devices, carried_in(): pieces = jax.tree.map(lambda part: lax.all_gather(part, axis), value)  41.2 us
    select_n x30, other arithmetic, hop(): jnp.where(position < mine, new, old)  33.7 us
    dot_general x36, matrix products, convolve(): jnp.dot(piece, weight[row_off, col_off], preferred_element_type=jnp.float32)  21 us
    all_gather x1, blocking collectives, carried_in(): pieces = jax.tree.map(lambda part: lax.all_gather(part, axis), value)  19.5 us
    ppermute x4, starting transfers between devices, extended(): lax.ppermute(lax.slice_in_dim(block, block.shape[dim] - width, None, axis...  14.3 us
    dynamic_update_slice x8, other arithmetic, shards(): _, local_states = lax.scan(advance, blank, (decay, drive))  14 us
    ppermute x4, starting transfers between devices, extended(): lax.ppermute(lax.slice_in_dim(block, 0, width, axis=dim), axis, backward)  8.08 us
  transfers between devices with their start and end apart: 11, of which 5 were waited for; matrix products, arithmetic and copies ran while one was open for 15% of the time, Pallas kernels for 0%

commit v1 on v0

v1 whole, which is shorter than its diff:
```python
import functools
import math

import jax
import jax.numpy as jnp
from jax import lax
from jax.experimental import pallas as pl
from jax.experimental.pallas import tpu as pltpu
from jax.sharding import PartitionSpec as P

MESH = pl.DeviceIdType.MESH
F32 = jnp.float32
BF16 = jnp.bfloat16


def kernel(
    dims,
    frames,
    cot,
    w_in,
    w_out,
    skip,
    log_decay,
    output,
    grad_frames,
    grad_in,
    grad_out,
    F, C, S, I,
    F3, C3, S3, I3,
    WOF, WIF,
    LS, LA, OB,
    DEC, DG,
    RF, EF, INF, RB, EB, INB,
    G, R0, R1, R2, A2, R3, O2, OUT,
    OB_F, OB_C,
    load_sem, halo_send, halo_recv, carry_send, carry_recv, ar_send, ar_recv, out_sem,
):
    nt, nx, ny, factor = dims
    T, R, W, CH = frames.shape
    n = nx
    pos = R * W
    piece = pos // nt
    half = 9 * CH
    group = half // 3
    chunk1, chunk2 = group // n, group // n // n

    tm = lax.axis_index("tm")
    tile = lax.axis_index("tile")
    ntile = ny * 2
    z, x = lax.div(tm, nx), lax.rem(tm, nx)
    y, core = lax.div(tile, 2), lax.rem(tile, 2)

    def on_tm(d):
        return (lax.rem(tm + d, nt), tile)

    def axis_peer(axis, d):
        if axis == "x":
            return (z * nx + lax.rem(x + d, nx), tile)
        if axis == "z":
            return (lax.rem(z + d, nt // nx) * nx + x, tile)
        return (tm, lax.rem(y + d, ny) * 2 + core)

    where_on = {"x": x, "y": y, "z": z}
    mate = (tm, y * 2 + 1 - core)

    barrier = pltpu.get_barrier_semaphore()
    for d in range(1, nt):
        pl.semaphore_signal(barrier, inc=1, device_id=on_tm(d), device_id_type=MESH)
    for d in range(1, ntile):
        pl.semaphore_signal(
            barrier, inc=1, device_id=(tm, lax.rem(tile + d, ntile)), device_id_type=MESH
        )

    load_f = pltpu.make_async_copy(frames, F.at[:, pl.ds(1, R)], load_sem.at[0])
    load_c = pltpu.make_async_copy(cot, C.at[:, pl.ds(1, R)], load_sem.at[1])
    load_f.start()
    load_c.start()

    @pl.when(tile == 0)
    def _():
        for field in (F, C, S, I):
            field[:, 0] = jnp.zeros((T, W, CH), BF16)

    @pl.when(tile == ntile - 1)
    def _():
        for field in (F, C, S, I):
            field[:, R + 1] = jnp.zeros((T, W, CH), BF16)

    DEC[...] = jnp.exp(log_decay[...])
    whole = DEC[0:1, :]
    for t in range(1, T):
        whole = whole * DEC[t : t + 1, :]
    DG[tm] = jnp.broadcast_to(whole, (8, CH))

    for i in range(3):
        for j in range(3):
            rows = pl.ds((i * 3 + j) * CH, CH)
            from_rows = pl.ds(((2 - i) * 3 + 2 - j) * CH, CH)
            WOF[rows, :] = w_out[from_rows, :].T
            WIF[rows, :] = w_in[from_rows, :].T

    load_f.wait()
    load_c.wait()
    pl.semaphore_wait(barrier, nt - 1 + ntile - 1)

    def halo(field, k):
        up = pltpu.make_async_remote_copy(
            field.at[:, pl.ds(1, 1)], field.at[:, pl.ds(R + 1, 1)],
            halo_send.at[k, 0], halo_recv.at[k, 0],
            device_id=(tm, lax.max(tile - 1, 0)), device_id_type=MESH,
        )
        down = pltpu.make_async_remote_copy(
            field.at[:, pl.ds(R, 1)], field.at[:, pl.ds(0, 1)],
            halo_send.at[k, 1], halo_recv.at[k, 1],
            device_id=(tm, lax.min(tile + 1, ntile - 1)), device_id_type=MESH,
        )

        def start():
            @pl.when(tile > 0)
            def _():
                up.start()

            @pl.when(tile < ntile - 1)
            def _():
                down.start()

        def wait_recv():
            @pl.when(tile < ntile - 1)
            def _():
                up.wait_recv()

            @pl.when(tile > 0)
            def _():
                down.wait_recv()

        def wait_send():
            @pl.when(tile > 0)
            def _():
                up.wait_send()

            @pl.when(tile < ntile - 1)
            def _():
                down.wait_send()

        return start, wait_recv, wait_send

    halos = [halo(field, k) for k, field in enumerate((F, C, S, I))]
    halos[0][0]()
    halos[1][0]()
    for d in range(1, nt):
        pltpu.make_async_remote_copy(
            DG.at[tm], DG.at[tm], carry_send.at[0], carry_recv.at[0],
            device_id=on_tm(d), device_id_type=MESH,
        ).start()

    col = lax.broadcasted_iota(jnp.int32, (1, W, CH), 1)

    def widen(src, dst, rows):
        def one(t, _):
            for r0, count in rows:
                v = src[t, r0 : r0 + count].astype(F32)
                left = jnp.where(col == 0, 0.0, pltpu.roll(v, 1, 1))
                right = jnp.where(col == W - 1, 0.0, pltpu.roll(v, W - 1, 1))
                dst[t, r0 : r0 + count, :, 0:CH] = left.astype(BF16)
                dst[t, r0 : r0 + count, :, CH : 2 * CH] = src[t, r0 : r0 + count]
                dst[t, r0 : r0 + count, :, 2 * CH : 3 * CH] = right.astype(BF16)
            return 0

        lax.fori_loop(0, T, one, 0)

    inner = [(r, 1) for r in range(1, R + 1)]
    outer = [(0, 1), (R + 1, 1)]

    def taps(src3, t):
        return jnp.concatenate(
            [src3[t, i : i + R].reshape(pos, 3 * CH) for i in range(3)], axis=-1
        )

    def conv(src3, t, weight):
        return jnp.dot(taps(src3, t), weight[...], preferred_element_type=F32)

    widen(F, F3, inner)
    widen(C, C3, inner)
    halos[0][1]()
    halos[1][1]()
    widen(F, F3, outer)
    widen(C, C3, outer)

    for t in range(T):
        rate = DEC[t : t + 1, :]
        inflow = (1.0 - rate) * conv(F3, t, w_in)
        if t:
            inflow = rate * LS[t - 1] + inflow
        LS[t] = inflow

    def exchange(src_of, dst_of, k):
        for d in range(1, nt):
            peer = on_tm(d)
            pltpu.make_async_remote_copy(
                src_of(peer[0]), dst_of(peer[0]), carry_send.at[k], carry_recv.at[k],
                device_id=peer, device_id_type=MESH,
            ).start()

    def all_but_one(ref, k, sems):
        part = ref.at[pl.ds(0, nt - 1)]
        pltpu.make_async_copy(part, part, sems.at[k]).wait()

    def rows_of(ref, k):
        return ref.at[pl.ds(pl.multiple_of(k * piece, piece), piece)]

    mine = pl.ds(pl.multiple_of(tm * piece, piece), piece)
    exchange(lambda p: rows_of(LS.at[T - 1], p), lambda p: RF.at[tm], 1)
    RF[tm] = LS[T - 1, mine, :]

    for t in reversed(range(T)):
        adjoint = conv(C3, t, WOF)
        if t < T - 1:
            adjoint = adjoint + OB[...]
        LA[t] = adjoint
        OB[...] = DEC[t : t + 1, :] * adjoint
    exchange(lambda p: rows_of(OB, p), lambda p: RB.at[tm], 2)
    RB[tm] = OB[mine, :]

    all_but_one(DG, 0, carry_recv)
    all_but_one(RF, 1, carry_recv)
    carry = jnp.zeros((piece, CH), F32)
    for k in range(nt):
        EF[k] = carry
        carry = DG[k, 0:1, :] * carry + RF[k]
    exchange(lambda p: EF.at[p], lambda p: rows_of(INF, tm), 3)
    INF[mine, :] = EF[tm]

    all_but_one(RB, 2, carry_recv)
    carry = jnp.zeros((piece, CH), F32)
    for k in reversed(range(nt)):
        EB[k] = carry
        carry = DG[k, 0:1, :] * carry + RB[k]
    exchange(lambda p: EB.at[p], lambda p: rows_of(INB, tm), 4)
    INB[mine, :] = EB[tm]

    def arrived(ref, k):
        part = ref.at[pl.ds(0, (nt - 1) * piece)]
        pltpu.make_async_copy(part, part, carry_recv.at[k]).wait()

    arrived(INF, 3)
    reach = None
    for t in range(T):
        rate = DEC[t : t + 1, :]
        reach = rate if reach is None else reach * rate
        S[t, 1 : R + 1] = (LS[t] + reach * INF[...]).astype(BF16).reshape(R, W, CH)
    halos[2][0]()

    def gram(own, src3):
        total = jnp.zeros((CH, 9 * CH), F32)
        for t in range(T):
            total = total + lax.dot_general(
                own[t, 1 : R + 1].reshape(pos, CH), taps(src3, t),
                (((0,), (0,)), ((), ())), preferred_element_type=F32,
            )
        return total

    total = gram(S, C3)
    for i in range(3):
        for j in range(3):
            k = (2 - i) * 3 + 2 - j
            G[half + (i * 3 + j) * CH : half + (i * 3 + j + 1) * CH, :] = total[:, k * CH : (k + 1) * CH]

    arrived(INB, 4)
    tail = None
    for t in reversed(range(T)):
        rate = DEC[t : t + 1, :]
        adjoint = LA[t] + (INB[...] if tail is None else tail * INB[...])
        I[t, 1 : R + 1] = ((1.0 - rate) * adjoint).astype(BF16).reshape(R, W, CH)
        tail = rate if tail is None else tail * rate
    halos[3][0]()
    total = gram(I, F3)
    for k in range(9):
        G[k * CH : (k + 1) * CH, :] = total[:, k * CH : (k + 1) * CH].T

    def conv_out(which, t):
        if which == 0:
            src3, weight, field, stage, dst = S3, w_out, F, OB_F, output
        else:
            src3, weight, field, stage, dst = I3, WIF, C, OB_C, grad_frames
        direct = skip[...] * field[t, 1 : R + 1].reshape(pos, CH).astype(F32)
        stage[t] = (conv(src3, t, weight) + direct).astype(BF16).reshape(R, W, CH)
        pltpu.make_async_copy(stage.at[t], dst.at[t], out_sem.at[which, t]).start()

    def fill(k):
        if k == 0:
            widen(S, S3, inner)
            halos[2][1]()
            widen(S, S3, outer)
        elif k == 1:
            for t in range(T):
                conv_out(0, t)
        elif k == 2:
            widen(I, I3, inner)
        elif k == 3:
            halos[3][1]()
            widen(I, I3, outer)
        elif k == 4:
            for t in range(T):
                conv_out(1, t)

    own_half = pl.multiple_of(core * half, half)
    mate_half = pl.multiple_of((1 - core) * half, half)
    core_rs = pltpu.make_async_remote_copy(
        G.at[pl.ds(mate_half, half)], R0, ar_send.at[0], ar_recv.at[0],
        device_id=mate, device_id_type=MESH,
    )
    core_rs.start()
    fill(0)
    core_rs.wait_recv()

    orders = (("x", "y", "z"), ("y", "z", "x"), ("z", "x", "y"))

    def total_wait(ref, sem):
        pltpu.make_async_copy(ref, ref, sem).wait()

    def add_block(g):
        rows = pl.ds(pl.multiple_of(own_half + g * group, chunk1), group)
        G[rows, :] = G[rows, :] + R0[g * group : (g + 1) * group, :]

    for g in range(3):
        add_block(g)
        a = orders[g][0]
        for d in range(1, n):
            q = lax.rem(where_on[a] + d, n)
            pltpu.make_async_remote_copy(
                G.at[pl.ds(pl.multiple_of(own_half + g * group + q * chunk1, chunk1), chunk1)],
                R1.at[g, d - 1], ar_send.at[1], ar_recv.at[1 + g],
                device_id=axis_peer(a, d), device_id_type=MESH,
            ).start()
    fill(1)
    for g in range(3):
        total_wait(R1.at[g], ar_recv.at[1 + g])
        a, b = orders[g][:2]
        p = where_on[a]
        rows = pl.ds(pl.multiple_of(own_half + g * group + p * chunk1, chunk1), chunk1)
        value = G[rows, :]
        for d in range(n - 1):
            value = value + R1[g, d]
        O2[g] = value
        for d in range(1, n):
            q = lax.rem(where_on[b] + d, n)
            pltpu.make_async_remote_copy(
                O2.at[g, pl.ds(pl.multiple_of(q * chunk2, chunk2), chunk2)],
                R2.at[g, d - 1], ar_send.at[2], ar_recv.at[4 + g],
                device_id=axis_peer(b, d), device_id_type=MESH,
            ).start()
    fill(2)
    for g in range(3):
        total_wait(R2.at[g], ar_recv.at[4 + g])
        b, c = orders[g][1:]
        p = where_on[b]
        value = O2[g, pl.ds(pl.multiple_of(p * chunk2, chunk2), chunk2), :]
        for d in range(n - 1):
            value = value + R2[g, d]
        A2[g] = value * factor
        r = where_on[c]
        R3[g, r] = A2[g]
        for d in range(1, n):
            pltpu.make_async_remote_copy(
                A2.at[g], R3.at[g, r], ar_send.at[3], ar_recv.at[7 + g],
                device_id=axis_peer(c, d), device_id_type=MESH,
            ).start()
    fill(3)
    part = R2
    total_wait(part, ar_send.at[2])
    for g in range(3):
        total_wait(R3.at[g, pl.ds(0, n - 1)], ar_recv.at[7 + g])
        b = orders[g][1]
        value = R3[g, 0]
        for k in range(1, n):
            value = value + R3[g, k]
        p = where_on[b]
        A2_rows = pl.ds(pl.multiple_of(p * chunk2, chunk2), chunk2)
        O2[3 + g, A2_rows, :] = value
        for d in range(1, n):
            pltpu.make_async_remote_copy(
                O2.at[3 + g, A2_rows], O2.at[3 + g, A2_rows], ar_send.at[4], ar_recv.at[10 + g],
                device_id=axis_peer(b, d), device_id_type=MESH,
            ).start()
    fill(4)
    for g in range(3):
        total_wait(O2.at[3 + g, pl.ds(0, (n - 1) * chunk2)], ar_recv.at[10 + g])
        a = orders[g][0]
        p = where_on[a]
        rows = pl.ds(pl.multiple_of(own_half + g * group + p * chunk1, chunk1), chunk1)
        OUT[rows, :] = O2[3 + g]
        for d in range(1, n):
            pltpu.make_async_remote_copy(
                OUT.at[rows], OUT.at[rows], ar_send.at[5], ar_recv.at[13 + g],
                device_id=axis_peer(a, d), device_id_type=MESH,
            ).start()
    mate_copies = []
    for g in range(3):
        rows = pl.ds(pl.multiple_of(own_half + g * group, group), group)
        total_wait(OUT.at[pl.ds(0, (n - 1) * chunk1)], ar_recv.at[13 + g])
        mate_copies.append(pltpu.make_async_remote_copy(
            OUT.at[rows], OUT.at[rows], ar_send.at[6 + g], ar_recv.at[16 + g],
            device_id=mate, device_id_type=MESH,
        ))
        mate_copies[-1].start()
    for copy in mate_copies:
        copy.wait_recv()
    finals = [
        pltpu.make_async_copy(OUT.at[0:half], grad_in, out_sem.at[2, 0]),
        pltpu.make_async_copy(OUT.at[half : 2 * half], grad_out, out_sem.at[2, 1]),
    ]
    for copy in finals:
        copy.start()

    for copy in mate_copies:
        copy.wait_send()
    core_rs.wait_send()
    total_wait(R1, ar_send.at[1])
    total_wait(R3.at[:, pl.ds(0, n - 1)], ar_send.at[3])
    total_wait(R2, ar_send.at[4])
    total_wait(R1, ar_send.at[5])
    for k in range(4):
        halos[k][2]()
    all_but_one(DG, 0, carry_send)
    for k in range(1, 5):
        all_but_one(RF, k, carry_send)
    for t in range(T):
        pltpu.make_async_copy(OB_F.at[t], output.at[t], out_sem.at[0, t]).wait()
        pltpu.make_async_copy(OB_C.at[t], grad_frames.at[t], out_sem.at[1, t]).wait()
    for copy in finals:
        copy.wait()


def solution(mesh):
    nt, ntile = mesh.shape["tm"], mesh.shape["tile"]
    nx = math.isqrt(nt)
    ny = ntile // 2

    def step(frames, cot, w_in, w_out, skip, log_decay):
        T, R, W, CH = frames.shape
        factor = 1.0 / math.sqrt(T * nt * R * ntile * W)
        pos = R * W
        piece = pos // nt
        n = nx
        half = 9 * CH
        group = half // 3
        c1, c2 = group // n, group // n // n
        vm = pltpu.VMEM
        field = vm((T, R + 2, W, CH), BF16)
        field3 = vm((T, R + 2, W, 3 * CH), BF16)
        dma = pltpu.SemaphoreType.DMA
        anyspace = pl.BlockSpec(memory_space=pl.ANY)
        vmem = pl.BlockSpec(memory_space=pltpu.VMEM)
        res = pl.pallas_call(
            functools.partial(kernel, (nt, nx, ny, factor)),
            out_shape=(
                jax.ShapeDtypeStruct(frames.shape, BF16),
                jax.ShapeDtypeStruct(frames.shape, BF16),
                jax.ShapeDtypeStruct((half, CH), F32),
                jax.ShapeDtypeStruct((half, CH), F32),
            ),
            in_specs=[anyspace, anyspace, vmem, vmem, vmem, vmem],
            out_specs=[anyspace] * 4,
            scratch_shapes=[
                field, field, field, field,
                field3, field3, field3, field3,
                vm((half, CH), BF16), vm((half, CH), BF16),
                vm((T, pos, CH), F32), vm((T, pos, CH), F32), vm((pos, CH), F32),
                vm((T, CH), F32), vm((nt, 8, CH), F32),
                vm((nt, piece, CH), F32), vm((nt, piece, CH), F32), vm((pos, CH), F32),
                vm((nt, piece, CH), F32), vm((nt, piece, CH), F32), vm((pos, CH), F32),
                vm((2 * half, CH), F32), vm((half, CH), F32),
                vm((3, n - 1, c1, CH), F32), vm((3, n - 1, c2, CH), F32), vm((3, c2, CH), F32),
                vm((3, n, c2, CH), F32), vm((6, c1, CH), F32), vm((2 * half, CH), F32),
                vm((T, R, W, CH), BF16), vm((T, R, W, CH), BF16),
                dma((2,)), dma((4, 2)), dma((4, 2)), dma((5,)), dma((5,)),
                dma((9,)), dma((19,)), dma((3, T)),
            ],
            compiler_params=pltpu.CompilerParams(
                collective_id=0, has_side_effects=True, vmem_limit_bytes=60 * 2**20
            ),
        )(
            frames, cot, w_in.reshape(half, CH), w_out.reshape(half, CH),
            skip.reshape(1, CH), log_decay,
        )
        return (res[0], res[1], res[2].reshape(3, 3, CH, CH), res[3].reshape(3, 3, CH, CH))

    block = P("tm", "tile", None, None)
    return jax.shard_map(
        step,
        mesh=mesh,
        in_specs=(block, block, P(), P(), P(), P("tm", None)),
        out_specs=(block, block, P(), P()),
        check_vma=False,
    )
```

time: 351 us -> 62.2 us (0.18)
  waiting for transfers between devices: 186 us -> 0 us
  other arithmetic: 61.5 us -> 0 us
  Pallas kernels: 0 us -> 56 us
  matrix products: 27.2 us -> 0 us
  starting transfers between devices: 22.5 us -> 0 us
  blocking collectives: 19.5 us -> 0 us
  between operations: 14.4 us -> 0.65 us
  local copies, waits for them, and re-layouts: 16.9 us -> 5.27 us
    psum x1 -> x0, waiting for transfers between devices: 141 us -> none  [shards(): in_summed, out_summed = lax.psum((in_partial, out_partial), ('tm', 'tile'))]
    pallas_call x0 -> x1, Pallas kernels: none -> 56 us  [step(): pl.pallas_call(functools.partial(kernel, (nt, nx, ny, factor)), out_shape...]
    all_gather x2 -> x0, waiting for transfers between devices: 41.2 us -> none  [carried_in(): pieces = jax.tree.map(lambda part: lax.all_gather(part, axis), value)]
    select_n x30 -> x0, other arithmetic: 33.7 us -> none  [hop(): jnp.where(position < mine, new, old)]
    dot_general x54 -> x0, matrix products: 27.2 us -> none  [the longest x36 21 us: convolve(): jnp.dot(piece, weight[row_off, col_off], preferred_element_type=jnp.float32)]
    ppermute x8 -> x0, starting transfers between devices: 22.3 us -> none  [the longest x4 14.3 us: extended(): lax.ppermute(lax.slice_in_dim(block, block.shape[dim] - width, None, axis...]
    all_gather x1 -> x0, blocking collectives: 19.5 us -> none  [carried_in(): pieces = jax.tree.map(lambda part: lax.all_gather(part, axis), value)]
    dynamic_update_slice x8 -> x0, other arithmetic: 14 us -> none  [shards(): _, local_states = lax.scan(advance, blank, (decay, drive))]
  transfers between devices with their start and end apart: 11 -> 0, of which waited for: 5 -> 0; matrix products, arithmetic and copies ran while one was open for 15% -> 0% of each run, Pallas kernels for 0% -> 0%
where the time goes in v1:
time: 62.2 us; the launch traced here: 62 us
  Pallas kernels  56 us (90%)
  local copies, waits for them, and re-layouts  5.27 us (8%)
  between operations  0.65 us (1%)
    pallas_call x1, Pallas kernels, step(): pl.pallas_call(functools.partial(kernel, (nt, nx, ny, factor)), out_shape...  56 us
    unnamed x10, local copies, waits for them, and re-layouts  5.27 us

profile of v1, /device:TPU:1, one launch (start us, length us, event | category | flops | bytes accessed | tf_op | source)
XLA Modules:
  0.0 62.0 jit_solution(12723562506047179071)
XLA Ops:
  0.6 56.0 %shard_map.93 = (bf16[4,8,64,128]{3,2,1,0:T(8,128)(2,1)}, bf16[4,8,64,128]{3,2,1,0:T(8,128)(2,1)}, f32[1152,128]{1,0:T(8,128)}, f32[1152,128]{1,0:T(8,128)}) custom-call(bf16[4,8,64,128]{3,2,1,0:T(8,128)(2,1)} %frames.1, bf16[4,8,64,128]{3,2,1,0:T(8,128)(2,1)} %cot.1, bf16[1152,128]{1,0:T(8,128)(2,1)} %bitcast.7, bf16[1152,128]{1,0:T(8,128)(2,1)} %bitcast.8, ...), custom_call_target="tpu_custom_call" | custom-call | tf_op jit(solution)/shard_map/pallas_call | solution.py:454
  56.7 0.0 copy-start.2
  56.7 1.9 %copy.14 = bf16[4,8,64,128]{3,2,1,0:T(8,128)(2,1)} copy(bf16[4,8,64,128]{3,2,1,0:T(8,128)(2,1)} %get-tuple-element.16) | data formatting | bytes 1048576
  58.6 0.0 copy-done.2
  58.6 0.0 copy-start.1
  58.6 0.8 %copy.15 = bf16[4,8,64,128]{3,2,1,0:T(8,128)(2,1)} copy(bf16[4,8,64,128]{3,2,1,0:T(8,128)(2,1)S(1)} %copy-done.2) | data formatting | bytes 1048576
  59.4 0.5 copy-done.1
  59.9 0.0 copy-start
  59.9 0.8 %copy.16 = f32[3,3,128,128]{3,2,1,0:T(8,128)} copy(f32[3,3,128,128]{3,2,1,0:T(8,128)S(1)} %bitcast.6) | data formatting | bytes 1179648
  60.7 0.5 copy-done
  61.2 0.8 %copy.17 = f32[3,3,128,128]{3,2,1,0:T(8,128)} copy(f32[3,3,128,128]{3,2,1,0:T(8,128)S(1)} %bitcast.5) | data formatting | bytes 1179648
Async XLA Ops:
  56.7 1.9 %copy-start.2 = (bf16[4,8,64,128]{3,2,1,0:T(8,128)(2,1)S(1)}, bf16[4,8,64,128]{3,2,1,0:T(8,128)(2,1)}, u32[]{:S(2)}) copy-start(bf16[4,8,64,128]{3,2,1,0:T(8,128)(2,1)} %get-tuple-element.17) | copy-start | bytes 1572868
  58.6 1.3 %copy-start.1 = (f32[1152,128]{1,0:T(8,128)S(1)}, f32[1152,128]{1,0:T(8,128)}, u32[]{:S(2)}) copy-start(f32[1152,128]{1,0:T(8,128)} %get-tuple-element.10) | copy-start | bytes 1769476
  59.9 1.3 %copy-start = (f32[1152,128]{1,0:T(8,128)S(1)}, f32[1152,128]{1,0:T(8,128)}, u32[]{:S(2)}) copy-start(f32[1152,128]{1,0:T(8,128)} %get-tuple-element.11) | copy-start | bytes 1769476
